TPU v7x, 32 devices: a whole 2x2x4 slice. The times are simulated.
32 devices in a mesh: dp: 8 (over z, x), ctx: 4 (over y, core).
Axes of the slice: x: 2, y: 2, z: 4, core: 2. Of those that a mesh axis runs over, the one named last changes fastest.
Arguments:
- inputs: bfloat16 [8, 512, 5376], P('dp', 'ctx'), may hold values from -6 to 6
- q_proj: bfloat16 [8, 512, 2048], P('dp', 'ctx'), may hold values from -260 to 260
- k_proj: bfloat16 [8, 512, 1024], P('dp', 'ctx'), may hold values from -260 to 260
- v_proj: bfloat16 [8, 512, 1024], P('dp', 'ctx'), may hold values from -6 to 6
- d_attn: bfloat16 [8, 512, 2048], P('dp', 'ctx'), may hold values from -6 to 6
- positions: int32 [8, 512], P('dp', 'ctx'), may hold values from 0 to 511, as said below
- windows: int32 [8], P('dp'), may hold values from 512 to 1024
- q_gain: float32 [128], replicated, may hold values from 0.7 to 5.5
- k_gain: float32 [128], replicated, may hold values from 0.7 to 5.5
- weight: bfloat16 [5376, 4096], P('dp'), may hold values from -0.078125 to 0.078125
Outputs:
- d_inputs: bfloat16 [8, 512, 5376], P('dp', 'ctx')
- d_weight_t: float32 [4096, 5376], P('ctx', 'dp')
- d_q_gain: float32 [128], replicated
- d_k_gain: float32 [128], replicated
Inputs may be any that keep to these rules, and one draw needn't show every extreme that they name: `positions`: within each sequence a position counts the tokens since its document began: it grows by one from token to token and falls to 0 where a document begins; the first token of a sequence has position 0. Some sequence holds a single document.
All inputs are finite; a program needn't handle non-finite values.
Results may differ from a plain program's by a relative error of at most 0.029.
Values may be sent and summed in bfloat16 or wider, within the bound.
A program may use at most 128 MiB of HBM per device.

v0:
```python
import math
import jax
import jax.numpy as jnp
from jax import lax
from jax.sharding import PartitionSpec as P

REACH = 8
score_scale = 168.0 ** (-0.5)
rope_base = 10000.0
norm_eps = 1e-06


def from_behind(value, axis, steps):
    count = lax.axis_size(axis)
    initial, last = (max(0, -steps), min(count, count - steps))
    return lax.ppermute(value, axis, [(source, source + steps) for source in range(initial, last)])


def rotated_unit(projected_rows, gain_vector, token_pos, head_count):
    head_width = gain_vector.shape[0]
    rows_heads = projected_rows.reshape(projected_rows.shape[0], head_count, head_width)
    inverse = lax.rsqrt(jnp.mean(rows_heads * rows_heads, axis=-1, keepdims=True) + norm_eps)
    normed = rows_heads * inverse * gain_vector
    half_width = head_width // 2
    frequency = jnp.exp(
        jnp.arange(half_width, dtype=jnp.float32) * (-2.0 * math.log(rope_base) / head_width)
    )
    angles = token_pos.astype(jnp.float32)[:, None] * frequency[None, :]
    cosine_table = jnp.cos(angles)[:, None, :]
    sine_table = jnp.sin(angles)[:, None, :]
    first_half = normed[..., :half_width]
    second_half = normed[..., half_width:]
    return jnp.concatenate(
        [
            first_half * cosine_table - second_half * sine_table,
            second_half * cosine_table + first_half * sine_table,
        ],
        axis=-1,
    )


def shards(inputs, q_proj, k_proj, v_proj, d_attn, positions, windows, q_gain, k_gain, weight):
    tok_rows = inputs.shape[1]
    head_width = q_gain.shape[0]
    query_heads = q_proj.shape[2] // head_width
    key_heads = k_proj.shape[2] // head_width
    group_size = query_heads // key_heads
    token_pos = positions[0]
    window = windows[0]
    input_cols = lax.all_to_all(inputs, "dp", split_axis=2, concat_axis=0, tiled=True)

    def query_side(projected_rows, gain_vector):
        return rotated_unit(projected_rows, gain_vector, token_pos, query_heads)

    def key_side(projected_rows, gain_vector):
        return rotated_unit(projected_rows, gain_vector, token_pos, key_heads)

    q_full, query_back = jax.vjp(query_side, q_proj[0].astype(jnp.float32), q_gain)
    k_full, key_back = jax.vjp(key_side, k_proj[0].astype(jnp.float32), k_gain)
    query_rotated = q_full.astype(jnp.bfloat16).reshape(tok_rows, key_heads, group_size, head_width)
    key_rotated = k_full.astype(jnp.bfloat16)
    v_own = v_proj[0].reshape(tok_rows, key_heads, head_width)
    reach_count = min(REACH, lax.axis_size("ctx") - 1)
    key_blocks = [key_rotated]
    value_blocks = [v_own]
    for distance_steps in range(1, reach_count + 1):
        far_keys, far_values = from_behind((key_rotated, v_own), "ctx", distance_steps)
        key_blocks.append(far_keys)
        value_blocks.append(far_values)
    all_keys = jnp.stack(key_blocks)
    all_values = jnp.stack(value_blocks)
    block_ids = jnp.arange(reach_count + 1, dtype=jnp.int32)
    offsets = jnp.arange(tok_rows, dtype=jnp.int32)
    distance = block_ids[None, :, None] * tok_rows + offsets[:, None, None] - offsets[None, None, :]
    allowed = (distance >= 0) & (distance < window) & (distance <= token_pos[:, None, None])
    scores = (
        jnp.einsum("ahgd,bchd->hgabc", query_rotated, all_keys, preferred_element_type=jnp.float32)
        * score_scale
    )
    scores = jnp.where(allowed, scores, -jnp.inf)
    row_max = jnp.max(scores, axis=(3, 4), keepdims=True)
    exponent = jnp.exp(scores - row_max)
    probs = exponent / jnp.sum(exponent, axis=(3, 4), keepdims=True)
    head_gradient = d_attn[0].reshape(tok_rows, key_heads, group_size, head_width)
    dprobs = jnp.einsum(
        "ahgd,bchd->hgabc", head_gradient, all_values, preferred_element_type=jnp.float32
    )
    delta = jnp.sum(probs * dprobs, axis=(3, 4), keepdims=True)
    dscores = (probs * (dprobs - delta)).astype(jnp.bfloat16)
    probs_low = probs.astype(jnp.bfloat16)
    dq_rot = (
        jnp.einsum("hgabc,bchd->ahgd", dscores, all_keys, preferred_element_type=jnp.float32)
        * score_scale
    )
    dk_blocks = (
        jnp.einsum("hgabc,ahgd->bchd", dscores, query_rotated, preferred_element_type=jnp.float32)
        * score_scale
    )
    dv_blocks = jnp.einsum(
        "hgabc,ahgd->bchd", probs_low, head_gradient, preferred_element_type=jnp.float32
    )
    dk_total = dk_blocks[0]
    dv_total = dv_blocks[0]
    for distance_steps in range(1, reach_count + 1):
        back_keys, back_values = from_behind(
            (
                dk_blocks[distance_steps].astype(jnp.bfloat16),
                dv_blocks[distance_steps].astype(jnp.bfloat16),
            ),
            "ctx",
            -distance_steps,
        )
        dk_total = dk_total + back_keys.astype(jnp.float32)
        dv_total = dv_total + back_values.astype(jnp.float32)
    dq_proj, dq_gain = query_back(dq_rot.reshape(tok_rows, query_heads, head_width))
    dk_proj, dk_gain = key_back(dk_total)
    dq_gain_all, dk_gain_all = lax.psum((dq_gain, dk_gain), ("dp", "ctx"))
    dv_proj = dv_total.reshape(tok_rows, key_heads * head_width)
    d_proj = jnp.concatenate([dq_proj, dk_proj, dv_proj], axis=-1).astype(jnp.bfloat16)[None]
    gathered = lax.all_gather(d_proj, "dp", axis=0, tiled=True)
    d_cols = jnp.einsum("btp,dp->btd", gathered, weight, preferred_element_type=jnp.float32)
    d_inputs = lax.all_to_all(
        d_cols.astype(jnp.bfloat16), "dp", split_axis=0, concat_axis=2, tiled=True
    )
    d_weight_t = lax.psum_scatter(
        jnp.einsum("btp,btd->pd", gathered, input_cols, preferred_element_type=jnp.float32).astype(
            jnp.bfloat16
        ),
        "ctx",
        scatter_dimension=0,
        tiled=True,
    ).astype(jnp.float32)
    return (d_inputs, d_weight_t, dq_gain_all, dk_gain_all)


def solution(mesh):
    placed = (
        P("dp", "ctx", None),
        P("dp", "ctx", None),
        P("dp", "ctx", None),
        P("dp", "ctx", None),
        P("dp", "ctx", None),
        P("dp", "ctx"),
        P("dp"),
        P(),
        P(),
        P("dp", None),
    )
    return jax.shard_map(
        shards,
        mesh=mesh,
        in_specs=placed,
        out_specs=(P("dp", "ctx", None), P("ctx", "dp"), P(), P()),
        check_vma=False,
    )
```

profile of v0, /device:TPU:0, one launch (start us, length us, event | category | flops | bytes accessed | tf_op | source)
XLA Modules:
  0.0 321.0 jit_solution(8718791477971543858)
XLA Ops:
  7.2 1.2 copy.176
  8.7 0.7 bitcast_convert_fusion.1
  9.4 0.3 multiply_cosine_fusion
  9.7 0.9 multiply_multiply_fusion.1
  10.6 0.3 subtract_convert_fusion.1
  10.8 0.9 pad_maximum_fusion.3
  11.7 5.0 %collective-permute-start.2 = (bf16[128,8,128]{2,0,1:T(8,128)(2,1)}, bf16[128,8,128]{2,0,1:T(8,128)(2,1)}, u32[]{:S(2)}, u32[]{:S(2)}) collective-permute-start(bf16[128,8,128]{2,0,1:T(8,128)(2,1)} %pad_maximum_fusion.3), channel_id=1, source_target_pairs={{0,3},{4,7},{8,11},{12,15},{16,19},{20,23},{24,27},{28,31}} | collective-permute-start | bytes 786440 | tf_op jit(solution)/shard_map/ppermute | solution.py:16
  16.7 2.0 collective-permute-start
  18.7 2.0 collective-permute-start.1
  20.8 0.8 copy.187
  21.7 2.0 collective-permute-start.3
  23.6 2.0 collective-permute-start.4
  25.9 0.3 multiply_reduce_fusion.2
  26.5 0.3 multiply_multiply_fusion
  26.8 0.5 subtract_convert_fusion
  28.5 1.4 reshape_squeeze.7
  29.9 1.2 copy.224
  31.4 1.5 collective-permute-start.5
  32.9 2.1 fusion.7
  35.0 0.9 fusion.6
  35.9 3.9 %collective-permute-done.5 = bf16[128,8,128]{2,0,1:T(8,128)(2,1)S(1)} collective-permute-done((bf16[128,8,128]{2,0,1:T(8,128)(2,1)}, bf16[128,8,128]{2,0,1:T(8,128)(2,1)S(1)}, u32[]{:S(2)}, u32[]{:S(2)}) %collective-permute-start.5) | collective-permute-done | bytes 262176 | tf_op jit(solution)/shard_map/ppermute | solution.py:16
  39.8 2.4 fusion.2
  42.2 1.3 fusion.4
  43.6 1.7 fusion.21
  45.2 2.2 fusion.57
  47.4 3.0 fusion.56
  50.5 1.4 copy.237
  51.9 1.4 copy.238
  53.3 0.9 slice_bitcast_fusion.7
  54.2 1.3 collective-permute-start.6
  55.5 1.3 collective-permute-start.7
  56.8 1.3 collective-permute-start.8
  58.1 1.8 multiply_add_fusion.1
  59.8 0.9 multiply_reduce_fusion
  60.9 1.8 fusion.22
  62.7 1.3 concatenate.51
  64.0 1.2 slice_bitcast_fusion.4
  65.2 1.3 collective-permute-start.10
  66.5 1.3 collective-permute-start.11
  67.8 1.3 collective-permute-start.9
  69.3 1.7 collective-permute-done.8
  71.0 1.4 fusion.40
  72.4 0.3 multiply_add_fusion.3
  72.7 0.5 multiply_reduce_fusion.3
  73.2 0.5 fusion.33
  74.0 2.3 collective-permute-done.10
  76.3 6.4 %collective-permute-done.11 = bf16[128,8,128]{0,2,1:T(8,128)(2,1)S(1)} collective-permute-done((bf16[128,8,128]{0,2,1:T(8,128)(2,1)S(1)}, bf16[128,8,128]{0,2,1:T(8,128)(2,1)S(1)}, u32[]{:S(2)}, u32[]{:S(2)}) %collective-permute-start.11) | collective-permute-done | bytes 262176 | tf_op jit(solution)/shard_map/ppermute | solution.py:16
  82.7 1.2 fusion.37
  84.0 1.0 pad_maximum_fusion.1
  85.1 0.3 reduce-scatter.2.cloned.1.call-start
  85.4 6.3 %copy.211 = bf16[1,128,5376]{1,0,2:T(2,128)(2,1)S(1)} copy(bf16[1,128,5376]{2,1,0:T(8,128)(2,1)} %param.10) | data formatting | bytes 2752512 | tf_op args[0]
  91.7 0.5 broadcast.142
  92.2 30.3 %reduce = bf16[5376,128]{1,0:T(8,128)(2,1)} reduce(bf16[5376,1,128]{2,1,0:T(2,128)(2,1)S(1)} %bitcast.178, bf16[]{:T(256)} %broadcast.142), dimensions={1}, to_apply=%bitcast.157.reduce_sub_computation | reduce | bytes 2752514
  122.4 3.2 %reshape.256 = bf16[8,2,43008]{2,1,0:T(2,128)(2,1)S(1)} reshape(bf16[5376,128]{1,0:T(8,128)(2,1)} %reduce) | data formatting | bytes 2752512
  125.7 71.0 %all_to_all.36 = bf16[8,2,43008]{2,1,0:T(2,128)(2,1)} all-to-all(bf16[8,2,43008]{2,1,0:T(2,128)(2,1)S(1)} %reshape.256), channel_id=1, replica_groups=mesh['dp'=8,'ctx'=4] {'dp'}, dimensions={0} | all-to-all | bytes 2752512 | tf_op jit(solution)/shard_map/all_to_all | solution.py:50
  196.7 4.5 %reshape.257 = bf16[5376,1,128]{2,1,0:T(2,128)(2,1)S(1)} reshape(bf16[8,2,43008]{2,1,0:T(2,128)(2,1)} %all_to_all.36) | data formatting | bytes 2752512
  201.2 1.3 copy.236
  202.5 29.1 %all-gather.2.cloned.1.call-done = bf16[8,128,4096]{2,1,0:T(8,128)(2,1)} async-done(((bf16[1,128,4096]{2,1,0:T(8,128)(2,1)}), bf16[8,128,4096]{2,1,0:T(8,128)(2,1)}) %all-gather.2.cloned.1.call-update) | async-done | bytes 8388624 | tf_op jit(solution)/shard_map/all_gather | solution.py:120
  231.6 10.2 %bitcast_convert_fusion = bf16[4096,672]{0,1:T(8,128)(2,1)} fusion(bf16[8,128,672]{1,2,0:T(8,128)(2,1)} %bitcast.192, bf16[8,128,4096]{2,1,0:T(8,128)(2,1)} %all-gather.2.cloned.1.call-done), kind=kOutput, calls=%fused_computation | convolution fusion | flops 5639897088 | bytes 15269888 | tf_op jit(solution)/shard_map/btp,btd->pd/dot_general | solution.py:126
  241.8 11.1 %fusion.18 = bf16[8,128,672]{1,2,0:T(8,128)(2,1)} fusion(bf16[8,128,4096]{2,1,0:T(8,128)(2,1)} %all-gather.2.cloned.1.call-done, bf16[672,4096]{1,0:T(8,128)(2,1)} %param.19), kind=kOutput, calls=%fused_computation.20 | convolution fusion | flops 5637832704 | bytes 15269888 | tf_op jit(solution)/shard_map/btp,dp->btd/dot_general | solution.py:121
  252.9 3.6 %all-to-all-start = ((bf16[8,128,672]{1,2,0:T(8,128)(2,1)}), bf16[8,128,672]{1,2,0:T(8,128)(2,1)S(1)}, u32[]{:S(2)}, u32[]{:S(2)}) async-start(bf16[8,128,672]{1,2,0:T(8,128)(2,1)} %fusion.18), calls=%async_computation | async-start | bytes 2752512 | tf_op jit(solution)/shard_map/all_to_all | solution.py:122
  256.4 53.0 %all-reduce.4 = (f32[128]{0:T(128)}, f32[128]{0:T(128)}) all-reduce(f32[128]{0:T(128)S(1)} %get-tuple-element.28, f32[128]{0:T(128)S(1)} %get-tuple-element.30), channel_id=1, replica_groups=mesh['dp'=8,'ctx'=4] {'dp','ctx'}, use_global_device_ids=true, to_apply=%region_9.10 | all-reduce | flops 256 | bytes 2048 | tf_op jit(solution)/shard_map/psum | solution.py:117
  309.5 1.5 copy.212
  311.0 3.2 %convert_element_type.126 = f32[1024,672]{0,1:T(8,128)} convert(bf16[1024,672]{0,1:T(8,128)(2,1)} %reduce-scatter.2.cloned.1.call-done) | non-fusion elementwise | flops 688128 | bytes 4128768 | tf_op jit(solution)/shard_map/convert_element_type | solution.py:132
  (54 shorter events, 2.7 us)
Async XLA Ops:
  7.2 13.5 %copy-start.4 = (bf16[1,128,1024]{2,1,0:T(8,128)(2,1)S(1)}, bf16[1,128,1024]{2,1,0:T(8,128)(2,1)}, u32[]{:S(2)}) copy-start(bf16[1,128,1024]{2,1,0:T(8,128)(2,1)} %param.13) | copy-start | bytes 786436
  7.2 18.5 %copy-start.2 = (bf16[1,128,2048]{2,1,0:T(8,128)(2,1)S(1)}, bf16[1,128,2048]{2,1,0:T(8,128)(2,1)}, u32[]{:S(2)}) copy-start(bf16[1,128,2048]{2,1,0:T(8,128)(2,1)} %param.11) | copy-start | bytes 1572868
  7.2 224.4 %all-gather.2.cloned.1.call-start = ((), (), s32[]{:S(2)}) async-start(), calls=%async_computation.3 | async-start | bytes 9437184 | tf_op jit(solution)/shard_map/all_gather | solution.py:120
  8.6 17.0 %copy-start = (f32[128,8,128]{2,0,1:T(8,128)}, f32[128,8,128]{2,0,1:T(8,128)S(1)}, u32[]{:S(2)}) copy-start(f32[128,8,128]{2,0,1:T(8,128)S(1)} %copy.177) | copy-start | bytes 1572868
  10.5 15.9 %copy-start.5 = (f32[128]{0:T(128)S(1)}, f32[128]{0:T(128)}, u32[]{:S(2)}) copy-start(f32[128]{0:T(128)} %param.17) | copy-start | bytes 1540
  11.7 19.7 %collective-permute-start.2 = (bf16[128,8,128]{2,0,1:T(8,128)(2,1)}, bf16[128,8,128]{2,0,1:T(8,128)(2,1)}, u32[]{:S(2)}, u32[]{:S(2)}) collective-permute-start(bf16[128,8,128]{2,0,1:T(8,128)(2,1)} %pad_maximum_fusion.3), channel_id=1, source_target_pairs={{0,3},{4,7},{8,11},{12,15},{16,19},{20,23},{24,27},{28,31}} | collective-permute-start | bytes 786440 | tf_op jit(solution)/shard_map/ppermute | solution.py:16
  16.7 16.2 %collective-permute-start = (bf16[128,8,128]{2,0,1:T(8,128)(2,1)}, bf16[128,8,128]{2,0,1:T(8,128)(2,1)}, u32[]{:S(2)}, u32[]{:S(2)}) collective-permute-start(bf16[128,8,128]{2,0,1:T(8,128)(2,1)} %pad_maximum_fusion.3), channel_id=1, source_target_pairs={{0,1},{1,2},{2,3},{4,5},{5,6},{6,7},{8,9},{9,10},{10,11},{12,13},{... | collective-permute-start | bytes 786440 | tf_op jit(solution)/shard_map/ppermute | solution.py:16
  18.7 14.3 %collective-permute-start.1 = (bf16[128,8,128]{2,0,1:T(8,128)(2,1)}, bf16[128,8,128]{2,0,1:T(8,128)(2,1)}, u32[]{:S(2)}, u32[]{:S(2)}) collective-permute-start(bf16[128,8,128]{2,0,1:T(8,128)(2,1)} %pad_maximum_fusion.3), channel_id=1, source_target_pairs={{0,2},{1,3},{4,6},{5,7},{8,10},{9,11},{12,14},{13,15},{16,18},{17,... | collective-permute-start | bytes 786440 | tf_op jit(solution)/shard_map/ppermute | solution.py:16
  21.7 14.2 %collective-permute-start.3 = (bf16[128,8,128]{2,0,1:T(8,128)(2,1)}, bf16[128,8,128]{2,0,1:T(8,128)(2,1)}, u32[]{:S(2)}, u32[]{:S(2)}) collective-permute-start(bf16[128,8,128]{2,0,1:T(8,128)(2,1)} %copy.187), channel_id=1, source_target_pairs={{0,1},{1,2},{2,3},{4,5},{5,6},{6,7},{8,9},{9,10},{10,11},{12,13},{... | collective-permute-start | bytes 786440 | tf_op jit(solution)/shard_map/ppermute | solution.py:16
  23.6 12.3 %collective-permute-start.4 = (bf16[128,8,128]{2,0,1:T(8,128)(2,1)}, bf16[128,8,128]{2,0,1:T(8,128)(2,1)}, u32[]{:S(2)}, u32[]{:S(2)}) collective-permute-start(bf16[128,8,128]{2,0,1:T(8,128)(2,1)} %copy.187), channel_id=1, source_target_pairs={{0,2},{1,3},{4,6},{5,7},{8,10},{9,11},{12,14},{13,15},{16,18},{17,... | collective-permute-start | bytes 786440 | tf_op jit(solution)/shard_map/ppermute | solution.py:16
  26.8 4.5 %copy-start.7 = (s32[1,128]{1,0:T(1,128)S(1)}, s32[1,128]{1,0:T(1,128)}, u32[]{:S(2)}) copy-start(s32[1,128]{1,0:T(1,128)} %param.15) | copy-start | bytes 1540
  31.4 8.4 %collective-permute-start.5 = (bf16[128,8,128]{2,0,1:T(8,128)(2,1)}, bf16[128,8,128]{2,0,1:T(8,128)(2,1)S(1)}, u32[]{:S(2)}, u32[]{:S(2)}) collective-permute-start(bf16[128,8,128]{2,0,1:T(8,128)(2,1)} %copy.187), channel_id=1, source_target_pairs={{0,3},{4,7},{8,11},{12,15},{16,19},{20,23},{24,27},{28,31}} | collective-permute-start | bytes 786440 | tf_op jit(solution)/shard_map/ppermute | solution.py:16
  35.0 4.8 %copy-start.3 = (bf16[128,8,2,128,1]{0,3,2,4,1:T(8,128)(2,1)S(1)}, bf16[128,8,2,128,1]{0,3,2,4,1:T(8,128)(2,1)}, u32[]{:S(2)}) copy-start(bf16[128,8,2,128,1]{0,3,2,4,1:T(8,128)(2,1)} %copy.224) | copy-start | bytes 1572868
  54.2 13.7 %collective-permute-start.6 = (bf16[128,8,128]{2,0,1:T(8,128)(2,1)}, bf16[128,8,128]{2,0,1:T(8,128)(2,1)}, u32[]{:S(2)}, u32[]{:S(2)}) collective-permute-start(bf16[128,8,128]{2,0,1:T(8,128)(2,1)} %get-tuple-element.40), channel_id=1, source_target_pairs={{1,0},{2,1},{3,2},{5,4},{6,5},{7,6},{9,8},{10,9},{11,10},{13,12},{... | collective-permute-start | bytes 786440 | tf_op jit(solution)/shard_map/ppermute | solution.py:16
  55.5 13.8 %collective-permute-start.7 = (bf16[128,8,128]{2,0,1:T(8,128)(2,1)}, bf16[128,8,128]{2,0,1:T(8,128)(2,1)}, u32[]{:S(2)}, u32[]{:S(2)}) collective-permute-start(bf16[128,8,128]{2,0,1:T(8,128)(2,1)} %get-tuple-element.42), channel_id=1, source_target_pairs={{2,0},{3,1},{6,4},{7,5},{10,8},{11,9},{14,12},{15,13},{18,16},{19,... | collective-permute-start | bytes 786440 | tf_op jit(solution)/shard_map/ppermute | solution.py:16
  56.8 14.2 %collective-permute-start.8 = (bf16[128,8,128]{2,0,1:T(8,128)(2,1)}, bf16[128,8,128]{2,0,1:T(8,128)(2,1)}, u32[]{:S(2)}, u32[]{:S(2)}) collective-permute-start(bf16[128,8,128]{2,0,1:T(8,128)(2,1)} %get-tuple-element.41), channel_id=1, source_target_pairs={{3,0},{7,4},{11,8},{15,12},{19,16},{23,20},{27,24},{31,28}} | collective-permute-start | bytes 786440 | tf_op jit(solution)/shard_map/ppermute | solution.py:16
  62.7 9.9 %copy-start.1 = (f32[128,8,128]{2,0,1:T(8,128)S(1)}, f32[128,8,128]{2,0,1:T(8,128)}, u32[]{:S(2)}) copy-start(f32[128,8,128]{2,0,1:T(8,128)} %copy-done) | copy-start | bytes 1572868
  62.7 9.9 %copy-start.6 = (f32[128]{0:T(128)S(1)}, f32[128]{0:T(128)}, u32[]{:S(2)}) copy-start(f32[128]{0:T(128)} %param.18) | copy-start | bytes 1540
  65.2 11.1 %collective-permute-start.10 = (bf16[128,8,128]{0,2,1:T(8,128)(2,1)S(1)}, bf16[128,8,128]{0,2,1:T(8,128)(2,1)S(1)}, u32[]{:S(2)}, u32[]{:S(2)}) collective-permute-start(bf16[128,8,128]{0,2,1:T(8,128)(2,1)S(1)} %get-tuple-element.45), channel_id=1, source_target_pairs={{2,0},{3,1},{6,4},{7,5},{10,8},{11,9},{14,12},{15,13},{18,16},{19,... | collective-permute-start | bytes 786440 | tf_op jit(solution)/shard_map/ppermute | solution.py:16
  66.5 16.2 %collective-permute-start.11 = (bf16[128,8,128]{0,2,1:T(8,128)(2,1)S(1)}, bf16[128,8,128]{0,2,1:T(8,128)(2,1)S(1)}, u32[]{:S(2)}, u32[]{:S(2)}) collective-permute-start(bf16[128,8,128]{0,2,1:T(8,128)(2,1)S(1)} %get-tuple-element.44), channel_id=1, source_target_pairs={{3,0},{7,4},{11,8},{15,12},{19,16},{23,20},{27,24},{31,28}} | collective-permute-start | bytes 786440 | tf_op jit(solution)/shard_map/ppermute | solution.py:16
  67.8 14.9 %collective-permute-start.9 = (bf16[128,8,128]{0,2,1:T(8,128)(2,1)S(1)}, bf16[128,8,128]{0,2,1:T(8,128)(2,1)S(1)}, u32[]{:S(2)}, u32[]{:S(2)}) collective-permute-start(bf16[128,8,128]{0,2,1:T(8,128)(2,1)S(1)} %get-tuple-element.43), channel_id=1, source_target_pairs={{1,0},{2,1},{3,2},{5,4},{6,5},{7,6},{9,8},{10,9},{11,10},{13,12},{... | collective-permute-start | bytes 786440 | tf_op jit(solution)/shard_map/ppermute | solution.py:16
  85.1 225.9 %reduce-scatter.2.cloned.1.call-start = ((), (), s32[]{:S(2)}) async-start(), calls=%async_computation.4 | async-start | bytes 6881280 | tf_op jit(solution)/shard_map/reduce_scatter | solution.py:125
  252.9 56.6 %all-to-all-start = ((bf16[8,128,672]{1,2,0:T(8,128)(2,1)}), bf16[8,128,672]{1,2,0:T(8,128)(2,1)S(1)}, u32[]{:S(2)}, u32[]{:S(2)}) async-start(bf16[8,128,672]{1,2,0:T(8,128)(2,1)} %fusion.18), calls=%async_computation | async-start | bytes 2752512 | tf_op jit(solution)/shard_map/all_to_all | solution.py:122
Sparse Core Ops, SparseCore 0:
  85.2 146.3 all-gather.1
  241.9 51.8 reduce-scatter.1
where the time goes:
time: 322 us; the launch traced here: 321 us
  blocking collectives  124 us (39%)
  other arithmetic  49.7 us (15%)
  waiting for transfers between devices  43.6 us (14%)
  matrix products  32.5 us (10%)
  local copies, waits for them, and re-layouts  30 us (9%)
  starting transfers between devices  26 us (8%)
  between operations  15.2 us (5%)
    all_to_all x1, blocking collectives, shards(): lax.all_to_all(inputs, 'dp', split_axis=2, concat_axis=0, tiled=True)  71 us
    psum x1, blocking collectives, shards(): dq_gain_all, dk_gain_all = lax.psum((dq_gain, dk_gain), ('dp', 'ctx'))  53 us
    unnamed x2, other arithmetic  30.4 us
    all_gather x1, waiting for transfers between devices, shards(): gathered = lax.all_gather(d_proj, 'dp', axis=0, tiled=True)  29.1 us
    ppermute x12, starting transfers between devices, from_behind(): lax.ppermute(value, axis, [(source, source + steps) for source in range(i...  22.2 us
    unnamed x27, local copies, waits for them, and re-layouts  21.7 us
    ppermute x12, waiting for transfers between devices, from_behind(): lax.ppermute(value, axis, [(source, source + steps) for source in range(i...  14.4 us
    dot_general x1, matrix products, shards(): jnp.einsum('btp,dp->btd', gathered, weight, preferred_element_type=jnp.fl...  11.1 us
  transfers between devices with their start and end apart: 15, of which 6 were waited for; matrix products, arithmetic and copies ran while one was open for 24% of the time, Pallas kernels for 0%

commit v1 on v0

--- a/solution.py
+++ b/solution.py
@@ -8,6 +8,23 @@
 score_scale = 168.0 ** (-0.5)
 rope_base = 10000.0
 norm_eps = 1e-06
+
+
+def laid_out(blocks, dim):
+    blocks = jnp.moveaxis(blocks, 0, dim)
+    shape = blocks.shape
+    return blocks.reshape(*shape[:dim], shape[dim] * shape[dim + 1], *shape[dim + 2 :])
+
+
+def ring_gather(x, axis, dim):
+    length = lax.axis_size(axis)
+    right = [(i, (i + 1) % length) for i in range(length)]
+    parts = [x]
+    while len(parts) < length:
+        parts.append(lax.ppermute(parts[-1], axis, right))
+    index = lax.axis_index(axis)
+    parts = jnp.stack(parts)[(index - jnp.arange(length)) % length]
+    return laid_out(parts, dim)
 
 
 def from_behind(value, axis, steps):
@@ -117,7 +134,7 @@
     dq_gain_all, dk_gain_all = lax.psum((dq_gain, dk_gain), ("dp", "ctx"))
     dv_proj = dv_total.reshape(tok_rows, key_heads * head_width)
     d_proj = jnp.concatenate([dq_proj, dk_proj, dv_proj], axis=-1).astype(jnp.bfloat16)[None]
-    gathered = lax.all_gather(d_proj, "dp", axis=0, tiled=True)
+    gathered = ring_gather(d_proj, "dp", 0)
     d_cols = jnp.einsum("btp,dp->btd", gathered, weight, preferred_element_type=jnp.float32)
     d_inputs = lax.all_to_all(
         d_cols.astype(jnp.bfloat16), "dp", split_axis=0, concat_axis=2, tiled=True

time: 322 us -> 418 us (1.30)
  waiting for transfers between devices: 43.6 us -> 154 us
  blocking collectives: 124 us -> 45.8 us
  starting transfers between devices: 26 us -> 75 us
  local copies, waits for them, and re-layouts: 30 us -> 47.2 us
    ppermute x0 -> x7, waiting for transfers between devices: none -> 136 us  [ring_gather(): parts.append(lax.ppermute(parts[-1], axis, right))]
    all_to_all x1 -> x0, blocking collectives: 71 us -> none  [shards(): lax.all_to_all(inputs, 'dp', split_axis=2, concat_axis=0, tiled=True)]
    ppermute x0 -> x7, starting transfers between devices: none -> 43 us  [ring_gather(): parts.append(lax.ppermute(parts[-1], axis, right))]
    all_gather x1 -> x0, waiting for transfers between devices: 29.1 us -> none  [shards(): gathered = lax.all_gather(d_proj, 'dp', axis=0, tiled=True)]
    unnamed x27 -> x58, local copies, waits for them, and re-layouts: 21.7 us -> 31.3 us
    gather x0 -> x1, local copies, waits for them, and re-layouts: none -> 8.16 us  [ring_gather(): parts = jnp.stack(parts)[(index - jnp.arange(length)) % length]]
    psum x1, blocking collectives: 53 us -> 45.8 us  [shards(): dq_gain_all, dk_gain_all = lax.psum((dq_gain, dk_gain), ('dp', 'ctx'))]
    all_to_all x0 -> x1, starting transfers between devices: none -> 5.99 us  [shards(): lax.all_to_all(inputs, 'dp', split_axis=2, concat_axis=0, tiled=True)]
  transfers between devices with their start and end apart: 15 -> 22, of which waited for: 6 -> 10; matrix products, arithmetic and copies ran while one was open for 24% -> 21% of each run, Pallas kernels for 0% -> 0%
where the time goes in v1:
time: 418 us; the launch traced here: 417 us
  waiting for transfers between devices  154 us (37%)
  starting transfers between devices  75 us (18%)
  local copies, waits for them, and re-layouts  47.2 us (11%)
  other arithmetic  46.5 us (11%)
  blocking collectives  45.8 us (11%)
  matrix products  32.9 us (8%)
  between operations  15.3 us (4%)
    ppermute x7, waiting for transfers between devices, ring_gather(): parts.append(lax.ppermute(parts[-1], axis, right))  136 us
    psum x1, blocking collectives, shards(): dq_gain_all, dk_gain_all = lax.psum((dq_gain, dk_gain), ('dp', 'ctx'))  45.8 us
    ppermute x7, starting transfers between devices, ring_gather(): parts.append(lax.ppermute(parts[-1], axis, right))  43 us
    unnamed x58, local copies, waits for them, and re-layouts  31.3 us
    unnamed x2, other arithmetic  31.3 us
    ppermute x12, starting transfers between devices, from_behind(): lax.ppermute(value, axis, [(source, source + steps) for source in range(i...  22.3 us
    ppermute x12, waiting for transfers between devices, from_behind(): lax.ppermute(value, axis, [(source, source + steps) for source in range(i...  17.7 us
    dot_general x1, matrix products, shards(): jnp.einsum('btp,dp->btd', gathered, weight, preferred_element_type=jnp.fl...  12.1 us
  transfers between devices with their start and end apart: 22, of which 10 were waited for; matrix products, arithmetic and copies ran while one was open for 21% of the time, Pallas kernels for 0%

profile of v1, /device:TPU:0, one launch (start us, length us, event | category | flops | bytes accessed | tf_op | source)
XLA Modules:
  0.0 416.6 jit_solution(13690136980927753644)
XLA Ops:
  7.2 1.2 copy.144
  10.1 0.9 multiply_multiply_fusion.1
  11.2 0.9 pad_maximum_fusion.3
  12.1 5.0 %collective-permute-start.2 = (bf16[128,8,128]{2,0,1:T(8,128)(2,1)}, bf16[128,8,128]{2,0,1:T(8,128)(2,1)}, u32[]{:S(2)}, u32[]{:S(2)}) collective-permute-start(bf16[128,8,128]{2,0,1:T(8,128)(2,1)} %pad_maximum_fusion.3), channel_id=1, source_target_pairs={{0,3},{4,7},{8,11},{12,15},{16,19},{20,23},{24,27},{28,31}} | collective-permute-start | bytes 786440 | tf_op jit(solution)/shard_map/ppermute | solution.py:33
  17.1 2.0 collective-permute-start
  19.1 2.0 collective-permute-start.1
  21.2 0.9 copy.156
  22.1 2.0 collective-permute-start.3
  24.1 2.0 collective-permute-start.4
  27.5 0.9 maximum_bitcast_fusion.2
  29.6 1.4 reshape_squeeze.7
  31.0 1.2 copy.190
  32.2 0.8 copy.159
  33.8 1.3 collective-permute-start.5
  35.2 2.1 fusion.7
  37.3 0.9 fusion.6
  38.2 2.0 collective-permute-done.5
  40.3 2.4 fusion.2
  42.7 1.3 fusion.4
  44.1 1.7 fusion.21
  46.6 2.6 fusion.57
  49.4 0.9 multiply_reduce_fusion
  50.4 1.3 collective-permute-start.6
  51.7 1.3 collective-permute-start.7
  53.0 1.3 collective-permute-start.8
  54.3 0.9 slice_bitcast_fusion.4
  55.2 1.4 collective-permute-start.10
  56.6 1.5 collective-permute-start.11
  58.4 1.3 collective-permute-start.9
  59.7 2.9 collective-permute-done.7
  62.6 5.9 %collective-permute-done.8 = bf16[128,8,128]{2,0,1:T(8,128)(2,1)S(1)} collective-permute-done((bf16[128,8,128]{2,0,1:T(8,128)(2,1)S(1)}, bf16[128,8,128]{2,0,1:T(8,128)(2,1)S(1)}, u32[]{:S(2)}, u32[]{:S(2)}) %collective-permute-start.8) | collective-permute-done | bytes 262176 | tf_op jit(solution)/shard_map/ppermute | solution.py:33
  70.2 6.8 %collective-permute-done.11 = bf16[128,8,128]{0,2,1:T(8,128)(2,1)} collective-permute-done((bf16[128,8,128]{0,2,1:T(8,128)(2,1)}, bf16[128,8,128]{0,2,1:T(8,128)(2,1)}, u32[]{:S(2)}, u32[]{:S(2)}) %collective-permute-start.11) | collective-permute-done | bytes 262176 | tf_op jit(solution)/shard_map/ppermute | solution.py:33
  76.9 1.3 fusion.37
  78.3 1.5 collective-permute-start.12
  79.9 23.4 %collective-permute-done.12 = bf16[1,128,4096]{1,2,0:T(8,128)(2,1)S(1)} collective-permute-done((bf16[1,128,4096]{1,2,0:T(8,128)(2,1)S(1)}, bf16[1,128,4096]{1,2,0:T(8,128)(2,1)S(1)}, u32[]{:S(2)}, u32[]{:S(2)}) %collective-permute-start.12) | collective-permute-done | bytes 1048608 | tf_op jit(solution)/shard_map/ppermute | solution.py:24
  103.3 24.1 %collective-permute-done.13 = bf16[1,128,4096]{1,2,0:T(8,128)(2,1)} collective-permute-done((bf16[1,128,4096]{1,2,0:T(8,128)(2,1)S(1)}, bf16[1,128,4096]{1,2,0:T(8,128)(2,1)}, u32[]{:S(2)}, u32[]{:S(2)}) %collective-permute-start.13) | collective-permute-done | bytes 1048608 | tf_op jit(solution)/shard_map/ppermute | solution.py:24
  127.3 6.3 %copy.176 = bf16[1,128,5376]{1,0,2:T(2,128)(2,1)S(1)} copy(bf16[1,128,5376]{2,1,0:T(8,128)(2,1)} %param.10) | data formatting | bytes 2752512 | tf_op args[0]
  134.1 30.3 %reduce = bf16[5376,128]{1,0:T(8,128)(2,1)} reduce(bf16[5376,1,128]{2,1,0:T(2,128)(2,1)S(1)} %bitcast.195, bf16[]{:T(256)} %broadcast.211), dimensions={1}, to_apply=%bitcast.172.reduce_sub_computation | reduce | bytes 2752514
  164.4 4.2 %reshape.368 = bf16[8,2,43008]{2,1,0:T(2,128)(2,1)} reshape(bf16[5376,128]{1,0:T(8,128)(2,1)} %reduce) | data formatting | bytes 2752512
  168.6 6.0 %all-to-all-start.1 = ((bf16[8,2,43008]{2,1,0:T(2,128)(2,1)}), bf16[8,2,43008]{2,1,0:T(2,128)(2,1)}, u32[]{:S(2)}, u32[]{:S(2)}) async-start(bf16[8,2,43008]{2,1,0:T(2,128)(2,1)} %reshape.368), calls=%async_computation.1 | async-start | bytes 2752512 | tf_op jit(solution)/shard_map/all_to_all | solution.py:67
  174.7 2.0 collective-permute-start.15
  176.7 1.1 maximum_dynamic-update-slice_fusion
  177.8 42.3 %collective-permute-done.15 = bf16[1,128,4096]{1,2,0:T(8,128)(2,1)} collective-permute-done((bf16[1,128,4096]{1,2,0:T(8,128)(2,1)}, bf16[1,128,4096]{1,2,0:T(8,128)(2,1)}, u32[]{:S(2)}, u32[]{:S(2)}) %collective-permute-start.15) | collective-permute-done | bytes 1048608 | tf_op jit(solution)/shard_map/ppermute | solution.py:24
  220.1 1.0 bitcast_dynamic-update-slice_fusion.6
  221.1 4.5 %reshape.369 = bf16[5376,1,128]{2,1,0:T(2,128)(2,1)S(1)} reshape(bf16[8,2,43008]{2,1,0:T(2,128)(2,1)} %all-to-all-done.1) | data formatting | bytes 2752512
  225.7 1.3 copy.204
  227.0 2.3 bitcast_dynamic-update-slice_fusion.5
  229.2 13.3 %collective-permute-done.16 = bf16[1,128,4096]{1,2,0:T(8,128)(2,1)} collective-permute-done((bf16[1,128,4096]{1,2,0:T(8,128)(2,1)}, bf16[1,128,4096]{1,2,0:T(8,128)(2,1)}, u32[]{:S(2)}, u32[]{:S(2)}) %collective-permute-start.16) | collective-permute-done | bytes 1048608 | tf_op jit(solution)/shard_map/ppermute | solution.py:24
  242.5 37.1 %collective-permute-start.17 = (bf16[1,128,4096]{1,2,0:T(8,128)(2,1)}, bf16[1,128,4096]{1,2,0:T(8,128)(2,1)S(1)}, u32[]{:S(2)}, u32[]{:S(2)}) collective-permute-start(bf16[1,128,4096]{1,2,0:T(8,128)(2,1)} %collective-permute-done.16), channel_id=1, source_target_pairs={{0,4},{4,8},{8,12},{12,16},{16,20},{20,24},{24,28},{28,0},{1,5},{5... | collective-permute-start | bytes 3145736 | tf_op jit(solution)/shard_map/ppermute | solution.py:24
  279.6 2.3 bitcast_dynamic-update-slice_fusion.4
  281.8 2.3 bitcast_dynamic-update-slice_fusion.3
  284.1 16.6 %collective-permute-done.17 = bf16[1,128,4096]{1,2,0:T(8,128)(2,1)S(1)} collective-permute-done((bf16[1,128,4096]{1,2,0:T(8,128)(2,1)}, bf16[1,128,4096]{1,2,0:T(8,128)(2,1)S(1)}, u32[]{:S(2)}, u32[]{:S(2)}) %collective-permute-start.17) | collective-permute-done | bytes 1048608 | tf_op jit(solution)/shard_map/ppermute | solution.py:24
  300.7 2.4 collective-permute-start.18
  303.1 2.3 bitcast_dynamic-update-slice_fusion.2
  305.4 1.0 bitcast_dynamic-update-slice_fusion.1
  306.4 16.6 %collective-permute-done.18 = bf16[1,128,4096]{1,2,0:T(8,128)(2,1)S(1)} collective-permute-done((bf16[1,128,4096]{1,2,0:T(8,128)(2,1)S(1)}, bf16[1,128,4096]{1,2,0:T(8,128)(2,1)S(1)}, u32[]{:S(2)}, u32[]{:S(2)}) %collective-permute-start.18) | collective-permute-done | bytes 1048608 | tf_op jit(solution)/shard_map/ppermute | solution.py:24
  323.0 1.1 bitcast_dynamic-update-slice_fusion
  324.2 8.2 %gather_fusion = bf16[8,128,4096]{1,2,0:T(8,128)(2,1)} fusion(bf16[8,128,4096]{1,2,0:T(8,128)(2,1)} %bitcast.64, s32[1024]{0:T(1024)S(1)} %pad_clamp_fusion), kind=kCustom, calls=%fused_computation | custom fusion | bytes 16777248 | tf_op jit(solution)/shard_map/gather | solution.py:26
  332.4 11.2 %bitcast_convert_fusion = bf16[4096,672]{0,1:T(8,128)(2,1)} fusion(bf16[8,128,4096]{1,2,0:T(8,128)(2,1)} %gather_fusion, bf16[8,128,672]{1,2,0:T(8,128)(2,1)S(1)} %bitcast.215), kind=kOutput, calls=%fused_computation.1 | convolution fusion | flops 5639897088 | bytes 15269888 | tf_op jit(solution)/shard_map/btp,btd->pd/dot_general | solution.py:143
  343.5 12.1 %fusion.18 = bf16[8,128,672]{1,2,0:T(8,128)(2,1)} fusion(bf16[8,128,4096]{1,2,0:T(8,128)(2,1)} %gather_fusion, bf16[672,4096]{1,0:T(8,128)(2,1)} %param.19), kind=kOutput, calls=%fused_computation.21 | convolution fusion | flops 5637832704 | bytes 15269888 | tf_op jit(solution)/shard_map/btp,dp->btd/dot_general | solution.py:138
  355.6 3.6 all-to-all-start
  359.2 45.8 %all-reduce.4 = (f32[128]{0:T(128)}, f32[128]{0:T(128)}) all-reduce(f32[128]{0:T(128)S(1)} %copy-done.21, f32[128]{0:T(128)S(1)} %get-tuple-element.26), channel_id=1, replica_groups=mesh['dp'=8,'ctx'=4] {'dp','ctx'}, use_global_device_ids=true, to_apply=%region_9.10 | all-reduce | flops 256 | bytes 2048 | tf_op jit(solution)/shard_map/psum | solution.py:134
  405.1 1.5 copy.178
  406.6 3.2 convert_element_type.133
  (96 shorter events, 8.4 us)
Async XLA Ops:
  7.2 13.9 %copy-start.12 = (bf16[1,128,1024]{2,1,0:T(8,128)(2,1)S(1)}, bf16[1,128,1024]{2,1,0:T(8,128)(2,1)}, u32[]{:S(2)}) copy-start(bf16[1,128,1024]{2,1,0:T(8,128)(2,1)} %param.13) | copy-start | bytes 786436
  7.2 18.9 %copy-start.9 = (bf16[1,128,2048]{2,1,0:T(8,128)(2,1)S(1)}, bf16[1,128,2048]{2,1,0:T(8,128)(2,1)}, u32[]{:S(2)}) copy-start(bf16[1,128,2048]{2,1,0:T(8,128)(2,1)} %param.11) | copy-start | bytes 1572868
  8.4 0.6 copy-start.16
  8.5 18.0 %copy-start.19 = (f32[128]{0:T(128)S(1)}, f32[128]{0:T(128)}, u32[]{:S(2)}) copy-start(f32[128]{0:T(128)} %param.17) | copy-start | bytes 1540
  9.0 17.6 %copy-start.14 = (f32[128,8]{0,1:T(8,128)}, f32[128,8]{0,1:T(8,128)S(1)}, u32[]{:S(2)}) copy-start(f32[128,8]{0,1:T(8,128)S(1)} %fusion.49) | copy-start | bytes 12292
  9.9 16.8 %copy-start.5 = (f32[128,64]{0,1:T(8,128)}, f32[128,64]{0,1:T(8,128)S(1)}, u32[]{:S(2)}) copy-start(f32[128,64]{0,1:T(8,128)S(1)} %get-tuple-element.44) | copy-start | bytes 98308
  9.9 16.8 %copy-start.7 = (f32[128,64]{0,1:T(8,128)}, f32[128,64]{0,1:T(8,128)S(1)}, u32[]{:S(2)}) copy-start(f32[128,64]{0,1:T(8,128)S(1)} %get-tuple-element.45) | copy-start | bytes 98308
  12.1 21.7 %collective-permute-start.2 = (bf16[128,8,128]{2,0,1:T(8,128)(2,1)}, bf16[128,8,128]{2,0,1:T(8,128)(2,1)}, u32[]{:S(2)}, u32[]{:S(2)}) collective-permute-start(bf16[128,8,128]{2,0,1:T(8,128)(2,1)} %pad_maximum_fusion.3), channel_id=1, source_target_pairs={{0,3},{4,7},{8,11},{12,15},{16,19},{20,23},{24,27},{28,31}} | collective-permute-start | bytes 786440 | tf_op jit(solution)/shard_map/ppermute | solution.py:33
  17.1 18.0 %collective-permute-start = (bf16[128,8,128]{2,0,1:T(8,128)(2,1)}, bf16[128,8,128]{2,0,1:T(8,128)(2,1)}, u32[]{:S(2)}, u32[]{:S(2)}) collective-permute-start(bf16[128,8,128]{2,0,1:T(8,128)(2,1)} %pad_maximum_fusion.3), channel_id=1, source_target_pairs={{0,1},{1,2},{2,3},{4,5},{5,6},{6,7},{8,9},{9,10},{10,11},{12,13},{... | collective-permute-start | bytes 786440 | tf_op jit(solution)/shard_map/ppermute | solution.py:33
  19.1 16.1 %collective-permute-start.1 = (bf16[128,8,128]{2,0,1:T(8,128)(2,1)}, bf16[128,8,128]{2,0,1:T(8,128)(2,1)}, u32[]{:S(2)}, u32[]{:S(2)}) collective-permute-start(bf16[128,8,128]{2,0,1:T(8,128)(2,1)} %pad_maximum_fusion.3), channel_id=1, source_target_pairs={{0,2},{1,3},{4,6},{5,7},{8,10},{9,11},{12,14},{13,15},{16,18},{17,... | collective-permute-start | bytes 786440 | tf_op jit(solution)/shard_map/ppermute | solution.py:33
  22.1 16.1 %collective-permute-start.3 = (bf16[128,8,128]{2,0,1:T(8,128)(2,1)}, bf16[128,8,128]{2,0,1:T(8,128)(2,1)}, u32[]{:S(2)}, u32[]{:S(2)}) collective-permute-start(bf16[128,8,128]{2,0,1:T(8,128)(2,1)} %copy.156), channel_id=1, source_target_pairs={{0,1},{1,2},{2,3},{4,5},{5,6},{6,7},{8,9},{9,10},{10,11},{12,13},{... | collective-permute-start | bytes 786440 | tf_op jit(solution)/shard_map/ppermute | solution.py:33
  24.1 14.1 %collective-permute-start.4 = (bf16[128,8,128]{2,0,1:T(8,128)(2,1)}, bf16[128,8,128]{2,0,1:T(8,128)(2,1)}, u32[]{:S(2)}, u32[]{:S(2)}) collective-permute-start(bf16[128,8,128]{2,0,1:T(8,128)(2,1)} %copy.156), channel_id=1, source_target_pairs={{0,2},{1,3},{4,6},{5,7},{8,10},{9,11},{12,14},{13,15},{16,18},{17,... | collective-permute-start | bytes 786440 | tf_op jit(solution)/shard_map/ppermute | solution.py:33
  33.8 6.4 %collective-permute-start.5 = (bf16[128,8,128]{2,0,1:T(8,128)(2,1)}, bf16[128,8,128]{2,0,1:T(8,128)(2,1)S(1)}, u32[]{:S(2)}, u32[]{:S(2)}) collective-permute-start(bf16[128,8,128]{2,0,1:T(8,128)(2,1)} %copy.156), channel_id=1, source_target_pairs={{0,3},{4,7},{8,11},{12,15},{16,19},{20,23},{24,27},{28,31}} | collective-permute-start | bytes 786440 | tf_op jit(solution)/shard_map/ppermute | solution.py:33
  37.3 3.0 copy-start.10
  37.3 3.0 copy-start.13
  42.7 1.4 copy-start.11
  46.6 2.7 copy-start.6
  46.6 2.7 copy-start.8
  46.6 2.8 copy-start.20
  50.4 18.5 %copy-start.15 = (f32[128,8]{0,1:T(8,128)S(1)}, f32[128,8]{0,1:T(8,128)}, u32[]{:S(2)}) copy-start(f32[128,8]{0,1:T(8,128)} %copy-done.14) | copy-start | bytes 12292
  50.4 18.5 %copy-start.18 = (f32[128]{0:T(128)S(1)}, f32[128]{0:T(128)}, u32[]{:S(2)}) copy-start(f32[128]{0:T(128)} %param.18) | copy-start | bytes 1540
  50.4 8.0 %collective-permute-start.6 = (bf16[128,8,128]{2,0,1:T(8,128)(2,1)S(1)}, bf16[128,8,128]{2,0,1:T(8,128)(2,1)S(1)}, u32[]{:S(2)}, u32[]{:S(2)}) collective-permute-start(bf16[128,8,128]{2,0,1:T(8,128)(2,1)S(1)} %get-tuple-element.34), channel_id=1, source_target_pairs={{1,0},{2,1},{3,2},{5,4},{6,5},{7,6},{9,8},{10,9},{11,10},{13,12},{... | collective-permute-start | bytes 786440 | tf_op jit(solution)/shard_map/ppermute | solution.py:33
  51.7 10.9 %collective-permute-start.7 = (bf16[128,8,128]{2,0,1:T(8,128)(2,1)S(1)}, bf16[128,8,128]{2,0,1:T(8,128)(2,1)S(1)}, u32[]{:S(2)}, u32[]{:S(2)}) collective-permute-start(bf16[128,8,128]{2,0,1:T(8,128)(2,1)S(1)} %get-tuple-element.36), channel_id=1, source_target_pairs={{2,0},{3,1},{6,4},{7,5},{10,8},{11,9},{14,12},{15,13},{18,16},{19,... | collective-permute-start | bytes 786440 | tf_op jit(solution)/shard_map/ppermute | solution.py:33
  53.0 15.5 %collective-permute-start.8 = (bf16[128,8,128]{2,0,1:T(8,128)(2,1)S(1)}, bf16[128,8,128]{2,0,1:T(8,128)(2,1)S(1)}, u32[]{:S(2)}, u32[]{:S(2)}) collective-permute-start(bf16[128,8,128]{2,0,1:T(8,128)(2,1)S(1)} %get-tuple-element.35), channel_id=1, source_target_pairs={{3,0},{7,4},{11,8},{15,12},{19,16},{23,20},{27,24},{31,28}} | collective-permute-start | bytes 786440 | tf_op jit(solution)/shard_map/ppermute | solution.py:33
  55.2 14.3 %copy-start.17 = (f32[128,8]{0,1:T(8,128)S(1)}, f32[128,8]{0,1:T(8,128)}, u32[]{:S(2)}) copy-start(f32[128,8]{0,1:T(8,128)} %copy-done.16) | copy-start | bytes 12292
  55.2 15.0 %collective-permute-start.10 = (bf16[128,8,128]{0,2,1:T(8,128)(2,1)}, bf16[128,8,128]{0,2,1:T(8,128)(2,1)}, u32[]{:S(2)}, u32[]{:S(2)}) collective-permute-start(bf16[128,8,128]{0,2,1:T(8,128)(2,1)} %get-tuple-element.39), channel_id=1, source_target_pairs={{2,0},{3,1},{6,4},{7,5},{10,8},{11,9},{14,12},{15,13},{18,16},{19,... | collective-permute-start | bytes 786440 | tf_op jit(solution)/shard_map/ppermute | solution.py:33
  56.6 20.3 %collective-permute-start.11 = (bf16[128,8,128]{0,2,1:T(8,128)(2,1)}, bf16[128,8,128]{0,2,1:T(8,128)(2,1)}, u32[]{:S(2)}, u32[]{:S(2)}) collective-permute-start(bf16[128,8,128]{0,2,1:T(8,128)(2,1)} %get-tuple-element.38), channel_id=1, source_target_pairs={{3,0},{7,4},{11,8},{15,12},{19,16},{23,20},{27,24},{31,28}} | collective-permute-start | bytes 786440 | tf_op jit(solution)/shard_map/ppermute | solution.py:33
  58.4 18.5 %collective-permute-start.9 = (bf16[128,8,128]{0,2,1:T(8,128)(2,1)}, bf16[128,8,128]{0,2,1:T(8,128)(2,1)S(1)}, u32[]{:S(2)}, u32[]{:S(2)}) collective-permute-start(bf16[128,8,128]{0,2,1:T(8,128)(2,1)} %get-tuple-element.37), channel_id=1, source_target_pairs={{1,0},{2,1},{3,2},{5,4},{6,5},{7,6},{9,8},{10,9},{11,10},{13,12},{... | collective-permute-start | bytes 786440 | tf_op jit(solution)/shard_map/ppermute | solution.py:33
  78.2 49.1 %copy-start = (bf16[128,8,128]{0,2,1:T(8,128)(2,1)}, bf16[128,8,128]{0,2,1:T(8,128)(2,1)S(1)}, u32[]{:S(2)}) copy-start(bf16[128,8,128]{0,2,1:T(8,128)(2,1)S(1)} %fusion.37) | copy-start | bytes 786436
  78.3 24.9 %collective-permute-start.12 = (bf16[1,128,4096]{1,2,0:T(8,128)(2,1)S(1)}, bf16[1,128,4096]{1,2,0:T(8,128)(2,1)S(1)}, u32[]{:S(2)}, u32[]{:S(2)}) collective-permute-start(bf16[1,128,4096]{1,2,0:T(8,128)(2,1)S(1)} %pad_maximum_fusion.1), channel_id=1, source_target_pairs={{0,4},{4,8},{8,12},{12,16},{16,20},{20,24},{24,28},{28,0},{1,5},{5... | collective-permute-start | bytes 3145736 | tf_op jit(solution)/shard_map/ppermute | solution.py:24
  103.3 24.1 %copy-start.3 = (bf16[1,128,4096]{1,2,0:T(8,128)(2,1)}, bf16[1,128,4096]{1,2,0:T(8,128)(2,1)S(1)}, u32[]{:S(2)}) copy-start(bf16[1,128,4096]{1,2,0:T(8,128)(2,1)S(1)} %collective-permute-done.12) | copy-start | bytes 3145732
  103.3 24.1 %collective-permute-start.13 = (bf16[1,128,4096]{1,2,0:T(8,128)(2,1)S(1)}, bf16[1,128,4096]{1,2,0:T(8,128)(2,1)}, u32[]{:S(2)}, u32[]{:S(2)}) collective-permute-start(bf16[1,128,4096]{1,2,0:T(8,128)(2,1)S(1)} %collective-permute-done.12), channel_id=1, source_target_pairs={{0,4},{4,8},{8,12},{12,16},{16,20},{20,24},{24,28},{28,0},{1,5},{5... | collective-permute-start | bytes 3145736 | tf_op jit(solution)/shard_map/ppermute | solution.py:24
  127.3 47.3 %collective-permute-start.14 = (bf16[1,128,4096]{1,2,0:T(8,128)(2,1)}, bf16[1,128,4096]{1,2,0:T(8,128)(2,1)}, u32[]{:S(2)}, u32[]{:S(2)}) collective-permute-start(bf16[1,128,4096]{1,2,0:T(8,128)(2,1)} %collective-permute-done.13), channel_id=1, source_target_pairs={{0,4},{4,8},{8,12},{12,16},{16,20},{20,24},{24,28},{28,0},{1,5},{5... | collective-permute-start | bytes 3145736 | tf_op jit(solution)/shard_map/ppermute | solution.py:24
  164.4 12.3 %copy-start.1 = (bf16[128,8,128]{0,2,1:T(8,128)(2,1)S(1)}, bf16[128,8,128]{0,2,1:T(8,128)(2,1)}, u32[]{:S(2)}) copy-start(bf16[128,8,128]{0,2,1:T(8,128)(2,1)} %copy-done) | copy-start | bytes 786436
  164.4 55.7 %copy-start.4 = (bf16[1,128,4096]{1,2,0:T(8,128)(2,1)S(1)}, bf16[1,128,4096]{1,2,0:T(8,128)(2,1)}, u32[]{:S(2)}) copy-start(bf16[1,128,4096]{1,2,0:T(8,128)(2,1)} %copy-done.3) | copy-start | bytes 3145732
  168.6 52.5 %all-to-all-start.1 = ((bf16[8,2,43008]{2,1,0:T(2,128)(2,1)}), bf16[8,2,43008]{2,1,0:T(2,128)(2,1)}, u32[]{:S(2)}, u32[]{:S(2)}) async-start(bf16[8,2,43008]{2,1,0:T(2,128)(2,1)} %reshape.368), calls=%async_computation.1 | async-start | bytes 2752512 | tf_op jit(solution)/shard_map/all_to_all | solution.py:67
  174.6 232.0 %reduce-scatter.2.cloned.1.call-start = ((), (), s32[]{:S(2)}) async-start(), calls=%async_computation.3 | async-start | bytes 6881280 | tf_op jit(solution)/shard_map/reduce_scatter | solution.py:142
  174.7 45.4 %collective-permute-start.15 = (bf16[1,128,4096]{1,2,0:T(8,128)(2,1)}, bf16[1,128,4096]{1,2,0:T(8,128)(2,1)}, u32[]{:S(2)}, u32[]{:S(2)}) collective-permute-start(bf16[1,128,4096]{1,2,0:T(8,128)(2,1)} %collective-permute-done.14), channel_id=1, source_target_pairs={{0,4},{4,8},{8,12},{12,16},{16,20},{20,24},{24,28},{28,0},{1,5},{5... | collective-permute-start | bytes 3145736 | tf_op jit(solution)/shard_map/ppermute | solution.py:24
  220.1 22.4 %collective-permute-start.16 = (bf16[1,128,4096]{1,2,0:T(8,128)(2,1)}, bf16[1,128,4096]{1,2,0:T(8,128)(2,1)}, u32[]{:S(2)}, u32[]{:S(2)}) collective-permute-start(bf16[1,128,4096]{1,2,0:T(8,128)(2,1)} %collective-permute-done.15), channel_id=1, source_target_pairs={{0,4},{4,8},{8,12},{12,16},{16,20},{20,24},{24,28},{28,0},{1,5},{5... | collective-permute-start | bytes 3145736 | tf_op jit(solution)/shard_map/ppermute | solution.py:24
  242.5 58.3 %collective-permute-start.17 = (bf16[1,128,4096]{1,2,0:T(8,128)(2,1)}, bf16[1,128,4096]{1,2,0:T(8,128)(2,1)S(1)}, u32[]{:S(2)}, u32[]{:S(2)}) collective-permute-start(bf16[1,128,4096]{1,2,0:T(8,128)(2,1)} %collective-permute-done.16), channel_id=1, source_target_pairs={{0,4},{4,8},{8,12},{12,16},{16,20},{20,24},{24,28},{28,0},{1,5},{5... | collective-permute-start | bytes 3145736 | tf_op jit(solution)/shard_map/ppermute | solution.py:24
  300.7 22.3 %collective-permute-start.18 = (bf16[1,128,4096]{1,2,0:T(8,128)(2,1)S(1)}, bf16[1,128,4096]{1,2,0:T(8,128)(2,1)S(1)}, u32[]{:S(2)}, u32[]{:S(2)}) collective-permute-start(bf16[1,128,4096]{1,2,0:T(8,128)(2,1)S(1)} %collective-permute-done.17), channel_id=1, source_target_pairs={{0,4},{4,8},{8,12},{12,16},{16,20},{20,24},{24,28},{28,0},{1,5},{5... | collective-permute-start | bytes 3145736 | tf_op jit(solution)/shard_map/ppermute | solution.py:24
  324.2 8.2 %copy-start.2 = (bf16[1,128,5376]{1,2,0:T(8,128)(2,1)S(1)}, bf16[1,128,5376]{1,2,0:T(8,128)(2,1)}, u32[]{:S(2)}) copy-start(bf16[1,128,5376]{1,2,0:T(8,128)(2,1)} %copy.204) | copy-start | bytes 4128772
  343.5 15.7 %copy-start.21 = (f32[128]{0:T(128)S(1)}, f32[128]{0:T(128)}, u32[]{:S(2)}) copy-start(f32[128]{0:T(128)} %get-tuple-element.24) | copy-start | bytes 1540
  355.6 49.4 %all-to-all-start = ((bf16[8,128,672]{1,2,0:T(8,128)(2,1)}), bf16[8,128,672]{1,2,0:T(8,128)(2,1)S(1)}, u32[]{:S(2)}, u32[]{:S(2)}) async-start(bf16[8,128,672]{1,2,0:T(8,128)(2,1)} %fusion.18), calls=%async_computation | async-start | bytes 2752512 | tf_op jit(solution)/shard_map/all_to_all | solution.py:139
Sparse Core Ops, SparseCore 0:
  343.7 50.8 reduce-scatter.1
